TPU v7x, 32 devices: a whole 2x2x4 slice. The times are simulated.
32 devices in a mesh: grp: 1, fsdp: 32 (over z, y, x, core), rep: 1.
Axes of the slice: x: 2, y: 2, z: 4, core: 2. Of those that a mesh axis runs over, the one named last changes fastest.
Arguments:
- items: bfloat16 [1, 16384, 512], P('rep', ('grp', 'fsdp')), may hold values from -30 to 30, as said below
- w_in: bfloat16 [512, 2048], P('fsdp'), may hold values from -0.25 to 0.25
- w_out: bfloat16 [2048, 1024], P('fsdp'), may hold values from -0.125 to 0.125
- users: bfloat16 [1, 1024, 1024], P('rep', ('grp', 'fsdp')), may hold values from -0.19921875 to 0.19921875
- res_codes: int32 [1, 16384, 1024], P('rep', ('grp', 'fsdp')), may hold values from 0 to 15
- range_idx: int32 [1024], P('grp'), may hold values from 0 to 3
- range_lo: float32 [4], P('grp'), may hold values from -1 to 1
- range_step: float32 [4], P('grp'), may hold values from 0.05 to 0.2
Outputs:
- new_codes: bfloat16 [1, 16384, 1024], P('rep', ('grp', 'fsdp'))
- best: float32 [1, 1024], P('rep', ('grp', 'fsdp'))
Inputs may be any that keep to these rules, and one draw needn't show every extreme that they name: `items`: item features of order one.
All inputs are finite; a program needn't handle non-finite values.
Results may differ from a plain program's by a relative error of at most 0.0075.
Values may be sent and summed in bfloat16 or wider, within the bound.
No kernel may reach another device: no remote copies, remote signals or barrier semaphores. Data moves between devices by JAX's collectives and lax.ppermute only.
A program may use at most 64 MiB of HBM per device.

v0:
```python
import jax
import jax.numpy as jnp
from jax import lax
from jax.sharding import PartitionSpec as P


def row_adder(left, piece):
    return jnp.dot(left, piece, preferred_element_type=jnp.float32)


def on_device(items, w_in, w_out, users, res_codes, range_idx, range_lo, range_step):
    features = items[0]
    first = row_adder(features, lax.all_gather(w_in, "fsdp", axis=0, tiled=True))
    hidden = jax.nn.silu(first).astype(jnp.bfloat16)
    embed = row_adder(hidden, lax.all_gather(w_out, "fsdp", axis=0, tiled=True))
    local_upper = jnp.max(embed, axis=0)
    local_lower = jnp.min(embed, axis=0)
    upper = lax.pmax(local_upper, ("fsdp", "rep"))
    lower = lax.pmin(local_lower, ("fsdp", "rep"))
    mid = (upper + lower) * 0.5
    half = (upper - lower) * 0.5
    new_codes = (7.5 * (embed - mid) / (half + 1e-05)).astype(jnp.bfloat16)[None]
    levels = jnp.arange(range_lo.shape[0], dtype=jnp.int32)
    match = (range_idx[None, :] == levels[:, None]).astype(jnp.float32)
    step_d = jnp.sum(range_step[:, None] * match, axis=0)
    lo_d = jnp.sum(range_lo[:, None] * match, axis=0)
    resident = res_codes[0].astype(jnp.bfloat16)
    member = lax.all_gather(users, "fsdp", axis=1, tiled=True)[0]
    folded = (member.astype(jnp.float32) * step_d).astype(jnp.bfloat16)
    offset = jnp.dot(member.astype(jnp.float32), lo_d, precision=lax.Precision.HIGHEST)
    scores = lax.dot_general(
        resident, folded, (((1,), (1,)), ((), ())), preferred_element_type=jnp.float32
    )
    local_best = (jnp.max(scores, axis=0) + offset)[None]
    merged = lax.pmax(local_best, "fsdp")
    count = users.shape[1]
    best = lax.dynamic_slice_in_dim(merged, lax.axis_index("fsdp") * count, count, 1)
    return (new_codes, best)


def solution(mesh):
    return jax.shard_map(
        on_device,
        mesh=mesh,
        in_specs=(
            P("rep", ("grp", "fsdp"), None),
            P("fsdp", None),
            P("fsdp", None),
            P("rep", ("grp", "fsdp"), None),
            P("rep", ("grp", "fsdp"), None),
            P("grp"),
            P("grp"),
            P("grp"),
        ),
        out_specs=(P("rep", ("grp", "fsdp"), None), P("rep", ("grp", "fsdp"))),
        check_vma=False,
    )
```

profile of v0, /device:TPU:0, one launch (start us, length us, event | category | flops | bytes accessed | tf_op | source)
XLA Modules:
  0.0 286.0 jit_solution(5587563280381236445)
XLA Ops:
  7.2 0.0 copy-start
  7.2 0.0 all-gather.8.cloned.1.call-start
  7.2 0.7 all-gather.8.cloned.1.call-update
  7.9 0.0 all-gather.4.cloned.1.call-start
  8.0 0.7 all-gather.4.cloned.1.call-update
  8.7 0.0 all-gather.6.cloned.1.call-start
  8.7 0.7 all-gather.6.cloned.1.call-update
  9.4 0.8 select_reduce_fusion
  10.2 59.8 %all-gather.8.cloned.1.call-done = bf16[1,1024,1024]{2,1,0:T(8,128)(2,1)} async-done(((bf16[1,32,1024]{2,1,0:T(8,128)(2,1)}), bf16[1,1024,1024]{2,1,0:T(8,128)(2,1)}) %all-gather.8.cloned.1.call-update) | async-done | bytes 2097168 | tf_op jit(solution)/shard_map/all_gather | solution.py:28
  70.0 0.0 copy-start.1
  70.0 3.5 %fusion.3 = f32[1,1024]{1,0:T(1,128)S(1)} fusion(f32[1024,1]{0,1:T(1,128)S(1)} %bitcast.29, bf16[1,1024,1024]{2,1,0:T(8,128)(2,1)} %all-gather.8.cloned.1.call-done), kind=kOutput, calls=%fused_computation.4 | convolution fusion | flops 12582912 | bytes 2105344 | tf_op jit(solution)/shard_map/dot_general | solution.py:30
  73.4 0.0 copy-done.1
  73.4 2.9 %fusion.7 = f32[1024]{0:T(1024)S(1)} fusion(bf16[1,1024,1024]{2,1,0:T(8,128)(2,1)S(1)} %copy-done.1, f32[1024]{0:T(1024)S(1)} %get-tuple-element.5, s32[1,512,1024]{2,1,0:T(8,128)} %param.12), kind=kOutput, calls=%fused_computation.9 | convolution fusion | flops 1077935104 | bytes 4202496 | tf_op jit(solution)/shard_map/dot_general | solution.py:31
  76.4 51.7 %all-gather.4.cloned.1.call-done = bf16[512,2048]{1,0:T(8,128)(2,1)} async-done(((bf16[16,2048]{1,0:T(8,128)(2,1)}), bf16[512,2048]{1,0:T(8,128)(2,1)}) %all-gather.4.cloned.1.call-update) | async-done | bytes 2097168 | tf_op jit(solution)/shard_map/all_gather | solution.py:13
  128.1 63.8 %all-gather.6.cloned.1.call-done = bf16[2048,1024]{1,0:T(8,128)(2,1)} async-done(((bf16[64,1024]{1,0:T(8,128)(2,1)}), bf16[2048,1024]{1,0:T(8,128)(2,1)}) %all-gather.6.cloned.1.call-update) | async-done | bytes 4194320 | tf_op jit(solution)/shard_map/all_gather | solution.py:15
  191.9 0.0 copy-done
  191.9 6.4 %fusion.20 = (f32[1024]{0:T(1024)S(1)}, f32[1024]{0:T(1024)S(1)}, f32[512,1024]{1,0:T(8,128)S(1)}) fusion(bf16[2048,1024]{1,0:T(8,128)(2,1)} %all-gather.6.cloned.1.call-done, bf16[512,2048]{1,0:T(8,128)(2,1)} %all-gather.4.cloned.1.call-done, bf16[1,512,512]{2,1,0:T(8,128)(2,1)S(1)} %copy-done), kind=kOutput, calls=%fused_computation.22 | convolution fusion | flops 3227514880 | bytes 8921088 | tf_op jit(solution)/shard_map/dot_general | solution.py:8
  198.3 39.2 %pmin.7 = f32[1024]{0:T(1024)S(1)} all-reduce(f32[1024]{0:T(1024)S(1)} %get-tuple-element.2), channel_id=1, replica_groups=mesh['grp'=1,'fsdp'=32,'rep'=1] {'fsdp','rep'}, use_global_device_ids=true, to_apply=%region_3.4 | all-reduce | flops 1024 | bytes 8192 | tf_op jit(solution)/shard_map/pmin | solution.py:19
  237.5 40.1 %all-reduce = (f32[1024]{0:T(1024)S(1)}, f32[1,1024]{1,0:T(1,128)S(1)}) all-reduce(f32[1024]{0:T(1024)S(1)} %get-tuple-element.3, f32[1,1024]{1,0:T(1,128)S(1)} %bitcast.30), channel_id=1, replica_groups=mesh['grp'=1,'fsdp'=32,'rep'=1] {'fsdp','rep'}, use_global_device_ids=true, to_apply=%region_1.2 | all-reduce | flops 2048 | bytes 16384 | tf_op jit(solution)/shard_map/pmax | solution.py:18
  277.6 0.6 constant_dynamic-slice_fusion
  278.2 1.3 fusion.12
  (2 shorter events, 0.0 us)
Async XLA Ops:
  7.2 184.7 %copy-start = (bf16[1,512,512]{2,1,0:T(8,128)(2,1)S(1)}, bf16[1,512,512]{2,1,0:T(8,128)(2,1)}, u32[]{:S(2)}) copy-start(bf16[1,512,512]{2,1,0:T(8,128)(2,1)} %param.8) | copy-start | bytes 1572868
  7.2 62.8 %all-gather.8.cloned.1.call-start = ((), (), s32[]{:S(2)}) async-start(), calls=%async_computation.2 | async-start | bytes 2162688 | tf_op jit(solution)/shard_map/all_gather | solution.py:28
  7.9 120.2 %all-gather.4.cloned.1.call-start = ((), (), s32[]{:S(2)}) async-start(), calls=%async_computation | async-start | bytes 2162688 | tf_op jit(solution)/shard_map/all_gather | solution.py:13
  8.7 183.2 %all-gather.6.cloned.1.call-start = ((), (), s32[]{:S(2)}) async-start(), calls=%async_computation.1 | async-start | bytes 4325376 | tf_op jit(solution)/shard_map/all_gather | solution.py:15
  70.0 3.5 %copy-start.1 = (bf16[1,1024,1024]{2,1,0:T(8,128)(2,1)S(1)}, bf16[1,1024,1024]{2,1,0:T(8,128)(2,1)}, u32[]{:S(2)}) copy-start(bf16[1,1024,1024]{2,1,0:T(8,128)(2,1)} %all-gather.8.cloned.1.call-done) | copy-start | bytes 6291460
Sparse Core Ops, SparseCore 0:
  10.9 59.0 all-gather.7
  72.8 55.2 all-gather.3
  131.0 60.8 all-gather.5
where the time goes:
time: 286 us
  waiting for transfers between devices  177 us (62%)
  blocking collectives  79.3 us (28%)
  between operations  13.8 us (5%)
  matrix products  12.8 us (4%)
    all_gather x1, waiting for transfers between devices, on_device(): embed = row_adder(hidden, lax.all_gather(w_out, 'fsdp', axis=0, tiled=True))  63.8 us
    all_gather x1, waiting for transfers between devices, on_device(): member = lax.all_gather(users, 'fsdp', axis=1, tiled=True)[0]  59.8 us
    all_gather x1, waiting for transfers between devices, on_device(): lax.all_gather(w_in, 'fsdp', axis=0, tiled=True)  51.7 us
    pmax x1, blocking collectives, on_device(): upper = lax.pmax(local_upper, ('fsdp', 'rep'))  40.1 us
    pmin x1, blocking collectives, on_device(): lower = lax.pmin(local_lower, ('fsdp', 'rep'))  39.2 us
    dot_general x1, matrix products, row_adder(): return jnp.dot(left, piece, preferred_element_type=jnp.float32)  6.45 us
  transfers between devices with their start and end apart: 3, of which 3 were waited for; matrix products, arithmetic and copies ran while one was open for 3% of the time, Pallas kernels for 0%

commit v1 on v0

--- a/solution.py
+++ b/solution.py
@@ -2,6 +2,18 @@
 import jax.numpy as jnp
 from jax import lax
 from jax.sharding import PartitionSpec as P
+
+
+def gather_by_bits(x, axis, dim):
+    ways, here = (lax.axis_size(axis), lax.axis_index(axis))
+    grown, reach = (x, 1)
+    while reach < ways:
+        theirs = lax.ppermute(grown, axis, [(d, d ^ reach) for d in range(ways)])
+        mine_first = jnp.concatenate([grown, theirs], axis=dim)
+        theirs_first = jnp.concatenate([theirs, grown], axis=dim)
+        grown = jnp.where(here & reach == 0, mine_first, theirs_first)
+        reach = 2 * reach
+    return grown
 
 
 def row_adder(left, piece):
@@ -10,7 +22,7 @@
 
 def on_device(items, w_in, w_out, users, res_codes, range_idx, range_lo, range_step):
     features = items[0]
-    first = row_adder(features, lax.all_gather(w_in, "fsdp", axis=0, tiled=True))
+    first = row_adder(features, gather_by_bits(w_in, "fsdp", 0))
     hidden = jax.nn.silu(first).astype(jnp.bfloat16)
     embed = row_adder(hidden, lax.all_gather(w_out, "fsdp", axis=0, tiled=True))
     local_upper = jnp.max(embed, axis=0)

time: 286 us -> 256 us (0.90)
  waiting for transfers between devices: 177 us -> 134 us
  starting transfers between devices: 0.11 us -> 9.25 us
    all_gather x1 -> x0, waiting for transfers between devices: 51.7 us -> none  [on_device(): lax.all_gather(w_in, 'fsdp', axis=0, tiled=True)]
    ppermute x0 -> x5, waiting for transfers between devices: none -> 23 us  [gather_by_bits(): theirs = lax.ppermute(grown, axis, [(d, d ^ reach) for d in range(ways)])]
    all_gather x1, waiting for transfers between devices: 59.8 us -> 50.5 us  [on_device(): member = lax.all_gather(users, 'fsdp', axis=1, tiled=True)[0]]
    ppermute x0 -> x5, starting transfers between devices: none -> 9.18 us  [gather_by_bits(): theirs = lax.ppermute(grown, axis, [(d, d ^ reach) for d in range(ways)])]
    all_gather x1, waiting for transfers between devices: 63.8 us -> 59.4 us  [on_device(): embed = row_adder(hidden, lax.all_gather(w_out, 'fsdp', axis=0, tiled=True))]
  transfers between devices with their start and end apart: 3 -> 7, of which waited for: 3 -> 6; matrix products, arithmetic and copies ran while one was open for 3% -> 3% of each run, Pallas kernels for 0% -> 0%
where the time goes in v1:
time: 256 us; the launch traced here: 255 us
  waiting for transfers between devices  134 us (52%)
  blocking collectives  79.3 us (31%)
  between operations  14.2 us (6%)
  matrix products  14 us (5%)
  starting transfers between devices  9.25 us (4%)
  other arithmetic  2.73 us (1%)
    all_gather x1, waiting for transfers between devices, on_device(): embed = row_adder(hidden, lax.all_gather(w_out, 'fsdp', axis=0, tiled=True))  59.4 us
    all_gather x1, waiting for transfers between devices, on_device(): member = lax.all_gather(users, 'fsdp', axis=1, tiled=True)[0]  50.5 us
    pmax x1, blocking collectives, on_device(): upper = lax.pmax(local_upper, ('fsdp', 'rep'))  40.1 us
    pmin x1, blocking collectives, on_device(): lower = lax.pmin(local_lower, ('fsdp', 'rep'))  39.2 us
    ppermute x5, waiting for transfers between devices, gather_by_bits(): theirs = lax.ppermute(grown, axis, [(d, d ^ reach) for d in range(ways)])  23 us
    ppermute x5, starting transfers between devices, gather_by_bits(): theirs = lax.ppermute(grown, axis, [(d, d ^ reach) for d in range(ways)])  9.18 us
    dot_general x1, matrix products, row_adder(): return jnp.dot(left, piece, preferred_element_type=jnp.float32)  7.63 us
  transfers between devices with their start and end apart: 7, of which 6 were waited for; matrix products, arithmetic and copies ran while one was open for 3% of the time, Pallas kernels for 0%

profile of v1, /device:TPU:0, one launch (start us, length us, event | category | flops | bytes accessed | tf_op | source)
XLA Modules:
  0.0 255.3 jit_solution(6096046822005243642)
XLA Ops:
  7.2 0.0 copy-start
  7.2 0.0 copy-start.3
  7.2 0.0 all-gather.5.cloned.1.call-start
  7.3 0.7 all-gather.5.cloned.1.call-update
  7.9 0.0 all-gather.3.cloned.1.call-start
  8.0 0.7 all-gather.3.cloned.1.call-update
  8.7 0.5 collective-permute-start
  9.2 1.1 collective-permute-done
  10.3 0.9 maximum_select_fusion.9
  11.3 2.9 %collective-permute-start.1 = (bf16[32,2048]{1,0:T(8,128)(2,1)S(1)}, bf16[32,2048]{1,0:T(8,128)(2,1)S(1)}, u32[]{:S(2)}, u32[]{:S(2)}) collective-permute-start(bf16[32,2048]{1,0:T(8,128)(2,1)S(1)} %maximum_select_fusion.9), channel_id=1, source_target_pairs={{0,2},{1,3},{2,0},{3,1},{4,6},{5,7},{6,4},{7,5},{8,10},{9,11},{10,... | collective-permute-start | bytes 393224 | tf_op jit(solution)/shard_map/ppermute | solution.py:11
  14.2 3.8 %collective-permute-done.1 = bf16[32,2048]{1,0:T(8,128)(2,1)S(1)} collective-permute-done((bf16[32,2048]{1,0:T(8,128)(2,1)S(1)}, bf16[32,2048]{1,0:T(8,128)(2,1)S(1)}, u32[]{:S(2)}, u32[]{:S(2)}) %collective-permute-start.1) | collective-permute-done | bytes 131104 | tf_op jit(solution)/shard_map/ppermute | solution.py:11
  18.1 1.8 collective-permute-start.2
  19.9 6.5 %collective-permute-done.2 = bf16[64,2048]{1,0:T(8,128)(2,1)S(1)} collective-permute-done((bf16[64,2048]{1,0:T(8,128)(2,1)S(1)}, bf16[64,2048]{1,0:T(8,128)(2,1)S(1)}, u32[]{:S(2)}, u32[]{:S(2)}) %collective-permute-start.2) | collective-permute-done | bytes 262176 | tf_op jit(solution)/shard_map/ppermute | solution.py:11
  26.4 0.1 maximum_select_fusion.7
  26.5 1.6 collective-permute-start.3
  28.1 11.5 %collective-permute-done.3 = bf16[128,2048]{1,0:T(8,128)(2,1)S(1)} collective-permute-done((bf16[128,2048]{1,0:T(8,128)(2,1)S(1)}, bf16[128,2048]{1,0:T(8,128)(2,1)S(1)}, u32[]{:S(2)}, u32[]{:S(2)}) %collective-permute-start.3) | collective-permute-done | bytes 524320 | tf_op jit(solution)/shard_map/ppermute | solution.py:11
  39.6 0.3 maximum_select_fusion.6
  39.9 2.4 collective-permute-start.4
  42.3 0.0 copy-done.3
  42.3 0.1 select_reduce_fusion
  42.4 50.5 %all-gather.5.cloned.1.call-done = bf16[1,1024,1024]{2,1,0:T(8,128)(2,1)} async-done(((bf16[1,32,1024]{2,1,0:T(8,128)(2,1)}), bf16[1,1024,1024]{2,1,0:T(8,128)(2,1)}) %all-gather.5.cloned.1.call-update) | async-done | bytes 2097168 | tf_op jit(solution)/shard_map/all_gather | solution.py:40
  92.9 3.5 %fusion.13 = f32[1,1024]{1,0:T(1,128)S(1)} fusion(f32[1024,1]{0,1:T(1,128)S(1)} %bitcast.41, bf16[1,1024,1024]{2,1,0:T(8,128)(2,1)} %all-gather.5.cloned.1.call-done), kind=kOutput, calls=%fused_computation.16 | convolution fusion | flops 12582912 | bytes 2105344 | tf_op jit(solution)/shard_map/dot_general | solution.py:42
  96.3 2.9 %fusion.19 = f32[1024]{0:T(1024)S(1)} fusion(bf16[1,1024,1024]{2,1,0:T(8,128)(2,1)S(1)} %copy-done.1, f32[1024]{0:T(1024)S(1)} %get-tuple-element.5, s32[1,512,1024]{2,1,0:T(8,128)} %param.12), kind=kOutput, calls=%fused_computation.22 | convolution fusion | flops 1077935104 | bytes 4202496 | tf_op jit(solution)/shard_map/dot_general | solution.py:43
  99.3 0.0 collective-permute-done.4
  99.3 0.0 copy-start.6
  99.3 1.0 copy-done.6
  100.3 59.4 %all-gather.3.cloned.1.call-done = bf16[2048,1024]{1,0:T(8,128)(2,1)} async-done(((bf16[64,1024]{1,0:T(8,128)(2,1)}), bf16[2048,1024]{1,0:T(8,128)(2,1)}) %all-gather.3.cloned.1.call-update) | async-done | bytes 4194320 | tf_op jit(solution)/shard_map/all_gather | solution.py:27
  159.7 7.6 %fusion.30 = (f32[1024]{0:T(1024)S(1)}, f32[1024]{0:T(1024)S(1)}, f32[512,1024]{1,0:T(8,128)S(1)}) fusion(bf16[2048,1024]{1,0:T(8,128)(2,1)} %all-gather.3.cloned.1.call-done, bf16[256,2048]{1,0:T(8,128)(2,1)} %copy-done.6, bf16[256,2048]{1,0:T(8,128)(2,1)} %copy-done.2, pred[]{:T(512)S(6)} %eq.28, bf16[1,512,512]{2,1,0:T(8,128)(2,1)S(1)} %copy-done), kind=kOutput, calls=%fused_computation.39 | convolution fusion | flops 3236952064 | bytes 8921089 | tf_op jit(solution)/shard_map/dot_general | solution.py:20
  167.3 39.2 %pmin.7 = f32[1024]{0:T(1024)S(1)} all-reduce(f32[1024]{0:T(1024)S(1)} %get-tuple-element.2), channel_id=1, replica_groups=mesh['grp'=1,'fsdp'=32,'rep'=1] {'fsdp','rep'}, use_global_device_ids=true, to_apply=%region_3.4 | all-reduce | flops 1024 | bytes 8192 | tf_op jit(solution)/shard_map/pmin | solution.py:31
  206.5 40.1 %all-reduce = (f32[1024]{0:T(1024)S(1)}, f32[1,1024]{1,0:T(1,128)S(1)}) all-reduce(f32[1024]{0:T(1024)S(1)} %get-tuple-element.3, f32[1,1024]{1,0:T(1,128)S(1)} %bitcast.42), channel_id=1, replica_groups=mesh['grp'=1,'fsdp'=32,'rep'=1] {'fsdp','rep'}, use_global_device_ids=true, to_apply=%region_1.2 | all-reduce | flops 2048 | bytes 16384 | tf_op jit(solution)/shard_map/pmax | solution.py:30
  246.6 0.6 constant_dynamic-slice_fusion
  247.2 1.3 fusion.24
  (12 shorter events, 0.1 us)
Async XLA Ops:
  7.2 152.5 %copy-start = (bf16[1,512,512]{2,1,0:T(8,128)(2,1)S(1)}, bf16[1,512,512]{2,1,0:T(8,128)(2,1)}, u32[]{:S(2)}) copy-start(bf16[1,512,512]{2,1,0:T(8,128)(2,1)} %param.8) | copy-start | bytes 1572868
  7.2 35.1 %copy-start.3 = (s32[1024]{0:T(1024)S(1)}, s32[1024]{0:T(1024)}, u32[]{:S(2)}) copy-start(s32[1024]{0:T(1024)} %param.13) | copy-start | bytes 12292
  7.2 35.1 %copy-start.4 = (f32[4]{0:T(128)S(1)}, f32[4]{0:T(128)}, u32[]{:S(2)}) copy-start(f32[4]{0:T(128)} %param.14) | copy-start | bytes 52
  7.2 35.1 %copy-start.5 = (f32[4]{0:T(128)S(1)}, f32[4]{0:T(128)}, u32[]{:S(2)}) copy-start(f32[4]{0:T(128)} %param.15) | copy-start | bytes 52
  7.2 85.7 %all-gather.5.cloned.1.call-start = ((), (), s32[]{:S(2)}) async-start(), calls=%async_computation.1 | async-start | bytes 2162688 | tf_op jit(solution)/shard_map/all_gather | solution.py:40
  7.9 151.7 %all-gather.3.cloned.1.call-start = ((), (), s32[]{:S(2)}) async-start(), calls=%async_computation | async-start | bytes 4325376 | tf_op jit(solution)/shard_map/all_gather | solution.py:27
  8.7 1.6 collective-permute-start
  11.3 6.7 %collective-permute-start.1 = (bf16[32,2048]{1,0:T(8,128)(2,1)S(1)}, bf16[32,2048]{1,0:T(8,128)(2,1)S(1)}, u32[]{:S(2)}, u32[]{:S(2)}) collective-permute-start(bf16[32,2048]{1,0:T(8,128)(2,1)S(1)} %maximum_select_fusion.9), channel_id=1, source_target_pairs={{0,2},{1,3},{2,0},{3,1},{4,6},{5,7},{6,4},{7,5},{8,10},{9,11},{10,... | collective-permute-start | bytes 393224 | tf_op jit(solution)/shard_map/ppermute | solution.py:11
  18.1 8.4 %collective-permute-start.2 = (bf16[64,2048]{1,0:T(8,128)(2,1)S(1)}, bf16[64,2048]{1,0:T(8,128)(2,1)S(1)}, u32[]{:S(2)}, u32[]{:S(2)}) collective-permute-start(bf16[64,2048]{1,0:T(8,128)(2,1)S(1)} %maximum_select_fusion.8), channel_id=1, source_target_pairs={{0,4},{1,5},{2,6},{3,7},{4,0},{5,1},{6,2},{7,3},{8,12},{9,13},{10,... | collective-permute-start | bytes 786440 | tf_op jit(solution)/shard_map/ppermute | solution.py:11
  26.5 13.1 %collective-permute-start.3 = (bf16[128,2048]{1,0:T(8,128)(2,1)S(1)}, bf16[128,2048]{1,0:T(8,128)(2,1)S(1)}, u32[]{:S(2)}, u32[]{:S(2)}) collective-permute-start(bf16[128,2048]{1,0:T(8,128)(2,1)S(1)} %maximum_select_fusion.7), channel_id=1, source_target_pairs={{0,8},{1,9},{2,10},{3,11},{4,12},{5,13},{6,14},{7,15},{8,0},{9,1},... | collective-permute-start | bytes 1572872 | tf_op jit(solution)/shard_map/ppermute | solution.py:11
  39.9 59.4 %copy-start.2 = (bf16[256,2048]{1,0:T(8,128)(2,1)}, bf16[256,2048]{1,0:T(8,128)(2,1)S(1)}, u32[]{:S(2)}) copy-start(bf16[256,2048]{1,0:T(8,128)(2,1)S(1)} %maximum_select_fusion.6) | copy-start | bytes 3145732
  39.9 59.4 %collective-permute-start.4 = (bf16[256,2048]{1,0:T(8,128)(2,1)S(1)}, bf16[256,2048]{1,0:T(8,128)(2,1)S(1)}, u32[]{:S(2)}, u32[]{:S(2)}) collective-permute-start(bf16[256,2048]{1,0:T(8,128)(2,1)S(1)} %maximum_select_fusion.6), channel_id=1, source_target_pairs={{0,16},{1,17},{2,18},{3,19},{4,20},{5,21},{6,22},{7,23},{8,24},{9,... | collective-permute-start | bytes 3145736 | tf_op jit(solution)/shard_map/ppermute | solution.py:11
  92.9 3.5 %copy-start.1 = (bf16[1,1024,1024]{2,1,0:T(8,128)(2,1)S(1)}, bf16[1,1024,1024]{2,1,0:T(8,128)(2,1)}, u32[]{:S(2)}) copy-start(bf16[1,1024,1024]{2,1,0:T(8,128)(2,1)} %all-gather.5.cloned.1.call-done) | copy-start | bytes 6291460
  99.3 1.0 copy-start.6
Sparse Core Ops, SparseCore 0:
  10.9 81.9 all-gather.4
  95.7 63.8 all-gather.2
